TPU v7x, 256 devices: a whole 4x4x8 slice. The times are simulated.
256 devices in a mesh: narrow: 8 (over y, z_lo), wide: 8 (over z_hi, core), nys: 4 (over x).
Axes of the slice: x: 4, y: 4, z: 8 (z_hi: 4, z_lo: 2; z = z_hi * 2 + z_lo), core: 2. Of those that a mesh axis runs over, the one named last changes fastest.
Arguments:
- centers: bfloat16 [262144, 1024], P(('narrow', 'wide', 'nys')), may hold values from -6 to 6
- weights: float32 [262144, 1000], P(('narrow', 'wide', 'nys')), may hold values from -6 to 6
- batch_points: bfloat16 [512, 1024], P(('narrow', 'wide', 'nys')), may hold values from -6 to 6
- labels: float32 [512, 1000], P(('narrow', 'wide', 'nys')), may hold values from -6 to 6
- nystrom_points: bfloat16 [2048, 1024], P(('narrow', 'nys')), may hold values from -6 to 6
- eigvecs: float32 [2048, 160], P(('narrow', 'nys')), may hold values from -0.125 to 0.125
- corrections: float32 [160], replicated, may hold values from 0.05 to 0.5
Outputs:
- new_weights: float32 [262144, 1000], P(('narrow', 'wide', 'nys'))
All inputs are finite; a program needn't handle non-finite values.
Results may differ from a plain program's by a relative error of at most 0.0003.
The roundings to bfloat16 on the way count: a program that leaves them out, or rounds other values in their place, can miss the bound.
Values may be sent and summed in bfloat16 or wider, within the bound.
A program may use at most 64 MiB of HBM per device.

v0:
```python
import math
import jax
import jax.numpy as jnp
from jax import lax
from jax.sharding import PartitionSpec as P

BATCH = 512
RATE = 16.0
SPREAD = 4.0


def kernel_with(left, left_sq, right):
    cross = lax.dot_general(
        left, right, (((1,), (1,)), ((), ())), preferred_element_type=jnp.float32
    )
    right_sq = jnp.sum(jnp.square(right.astype(jnp.float32)), axis=1)
    dist = jnp.sqrt(jnp.maximum(left_sq[:, None] + right_sq[None, :] - 2.0 * cross, 0.0))
    radius = math.sqrt(2.0 * left.shape[1])
    return jnp.exp((radius - dist) / SPREAD).astype(jnp.bfloat16)


def squares(points):
    return jnp.sum(jnp.square(points.astype(jnp.float32)), axis=1)


def per_device(centers, weights, batch_points, labels, nystrom_points, eigvecs, corrections):
    batch_all = lax.all_gather(batch_points, ("narrow", "wide", "nys"), axis=0, tiled=True)
    count = lax.axis_size(("narrow", "wide", "nys"))
    scale = (centers.shape[0] * count) ** (-0.5)
    center_sq = squares(centers)
    k_batch = kernel_with(centers, center_sq, batch_all)
    partial_value = (
        lax.dot_general(
            k_batch,
            weights.astype(jnp.bfloat16),
            (((0,), (0,)), ((), ())),
            preferred_element_type=jnp.float32,
        )
        * scale
    )
    rows = labels.shape[0]
    offset = lax.axis_index(("narrow", "wide", "nys")) * rows
    placed = lax.dynamic_update_slice(jnp.zeros_like(partial_value), labels, (offset, jnp.int32(0)))
    residual = lax.psum(partial_value - placed, ("narrow", "wide", "nys")).astype(jnp.bfloat16)
    k_nystrom = kernel_with(nystrom_points, squares(nystrom_points), batch_all)
    pulled = jnp.dot(k_nystrom, residual, preferred_element_type=jnp.float32)
    local_proj = lax.dot_general(
        eigvecs, pulled, (((0,), (0,)), ((), ())), precision=lax.Precision.HIGHEST
    )
    projected = lax.psum(local_proj, ("narrow", "nys"))
    scaled_proj = corrections[:, None] * projected
    gradient = jnp.dot(k_batch, residual, preferred_element_type=jnp.float32)
    corrected = jnp.dot(eigvecs, scaled_proj, precision=lax.Precision.HIGHEST).astype(jnp.bfloat16)
    points = lax.all_gather(nystrom_points, ("narrow", "nys"), axis=0, tiled=True)
    coefs = lax.all_gather(corrected, ("narrow", "nys"), axis=0, tiled=True)
    tile = kernel_with(centers, center_sq, points)
    nystrom_term = jnp.dot(tile, coefs, preferred_element_type=jnp.float32)
    return weights - RATE / BATCH * (gradient - nystrom_term)


def solution(mesh):
    placed = (
        P(("narrow", "wide", "nys"), None),
        P(("narrow", "wide", "nys"), None),
        P(("narrow", "wide", "nys"), None),
        P(("narrow", "wide", "nys"), None),
        P(("narrow", "nys"), None),
        P(("narrow", "nys"), None),
        P(),
    )
    return jax.shard_map(
        per_device,
        mesh=mesh,
        in_specs=placed,
        out_specs=P(("narrow", "wide", "nys"), None),
        check_vma=False,
    )
```

profile of v0, /device:TPU:2, one launch (start us, length us, event | category | flops | bytes accessed | tf_op | source)
XLA Modules:
  0.0 1286.6 jit_solution(18334620316952581570)
XLA Ops:
  6.5 0.0 copy-start
  6.5 0.0 all-gather.9.cloned.1.call-start
  6.5 0.7 all-gather.9.cloned.1.call-update
  7.3 0.0 all-reduce.3.cloned.1.call-start
  7.3 0.9 copy.9
  8.2 0.2 broadcast_in_dim.2
  8.5 6.3 dynamic_update_slice.3
  14.8 1.0 multiply_reduce_fusion.3
  15.8 2.1 multiply_reduce_fusion.1
  17.9 523.6 %all-gather.9.cloned.1.call-done = bf16[256,2,1024]{2,1,0:T(2,128)(2,1)} async-done(((bf16[1,2,1024]{2,1,0:T(2,128)(2,1)}), bf16[256,2,1024]{2,1,0:T(2,128)(2,1)}) %all-gather.9.cloned.1.call-update) | async-done | bytes 1048592 | tf_op jit(solution)/shard_map/all_gather | solution.py:27
  541.5 1.5 reshape.6
  543.0 0.3 multiply_reduce_fusion.2
  543.3 0.0 copy-start.1
  543.3 3.8 exponential_convert_fusion.1
  547.1 0.0 copy-start.2
  547.1 1.1 copy-done.2
  548.2 0.0 copy-done.1
  548.2 0.0 copy-start.4
  548.2 2.6 multiply_subtract_fusion.1
  550.7 0.0 copy-start.5
  550.7 81.6 %all-reduce.4 = bf16[512,1000]{0,1:T(8,128)(2,1)S(1)} all-reduce(f32[512,1000]{0,1:T(8,128)} %multiply_subtract_fusion.1), channel_id=1, replica_groups=mesh['narrow'=8,'wide'=8,'nys'=4] {'narrow','wide','nys'}, use_global_device_ids=true, to_apply=%region_2.0 | all-reduce | flops 512000 | bytes 3072000 | tf_op jit(solution)/shard_map/psum | solution.py:44
  632.3 0.0 copy-done.4
  632.3 0.8 fusion.12
  633.2 0.0 copy-done
  633.2 1.6 convolution_bitcast_fusion
  634.7 0.0 all-reduce.3.cloned.1.call-update
  634.7 0.0 all-gather.5.cloned.1.call-start
  634.8 0.7 all-gather.5.cloned.1.call-update
  635.5 0.2 all-gather.7.cloned.1.call-start
  635.7 301.3 %all-reduce.3.cloned.1.call-done = f32[160,1000]{1,0:T(8,128)} async-done(((f32[160,1000]{1,0:T(8,128)}), f32[160,1000]{1,0:T(8,128)}) %all-reduce.3.cloned.1.call-update) | async-done | bytes 640016 | tf_op jit(solution)/shard_map/psum | solution.py:50
  937.0 0.0 copy-done.5
  937.0 2.3 fusion.4
  939.4 0.0 all-gather.7.cloned.1.call-update
  939.4 157.5 %all-gather.5.cloned.1.call-done = bf16[2048,1024]{1,0:T(8,128)(2,1)} async-done(((bf16[64,1024]{1,0:T(8,128)(2,1)}), bf16[2048,1024]{1,0:T(8,128)(2,1)}) %all-gather.5.cloned.1.call-update) | async-done | bytes 4194320 | tf_op jit(solution)/shard_map/all_gather | solution.py:54
  1097.0 3.1 multiply_reduce_fusion
  1100.0 0.0 copy-start.3
  1100.1 157.9 %all-gather.7.cloned.1.call-done = bf16[2048,1000]{1,0:T(8,128)(2,1)} async-done(((bf16[64,1000]{1,0:T(8,128)(2,1)}), bf16[2048,1000]{1,0:T(8,128)(2,1)}) %all-gather.7.cloned.1.call-update) | async-done | bytes 4096016 | tf_op jit(solution)/shard_map/all_gather | solution.py:55
  1258.0 15.5 %fusion.13 = f32[1024,1000]{0,1:T(8,128)} fusion(bf16[2048,1000]{1,0:T(8,128)(2,1)} %all-gather.7.cloned.1.call-done, bf16[1024,1024]{1,0:T(8,128)(2,1)} %param.7, bf16[2048,1024]{1,0:T(8,128)(2,1)} %all-gather.5.cloned.1.call-done, f32[2048]{0:T(1024)S(1)} %multiply_reduce_fusion, f32[1024]{0:T(1024)S(1)} %multiply_reduce_fusion.1), kind=kOutput, calls=%fused_computation.21 | convolution fusion | flops 8503951360 | bytes 14495744 | tf_op jit(solution)/shard_map/dot_general | solution.py:57
  1273.5 0.0 copy-done.3
  1273.5 6.7 multiply_subtract_fusion
Async XLA Ops:
  6.5 626.6 %copy-start = (f32[64,160]{1,0:T(8,128)S(1)}, f32[64,160]{1,0:T(8,128)}, u32[]{:S(2)}) copy-start(f32[64,160]{1,0:T(8,128)} %param.12) | copy-start | bytes 122884
  6.5 535.0 %all-gather.9.cloned.1.call-start = ((), (), s32[]{:S(2)}) async-start(), calls=%async_computation.3 | async-start | bytes 1052672 | tf_op jit(solution)/shard_map/all_gather | solution.py:27
  7.3 929.8 %all-reduce.3.cloned.1.call-start = ((), (), s32[]{:S(2)}) async-start(), calls=%async_computation.1 | async-start | bytes 1310720 | tf_op jit(solution)/shard_map/psum | solution.py:50
  543.3 4.9 copy-start.1
  547.1 1.1 copy-start.2
  548.2 84.1 %copy-start.4 = (bf16[64,1024]{1,0:T(8,128)(2,1)S(1)}, bf16[64,1024]{1,0:T(8,128)(2,1)}, u32[]{:S(2)}) copy-start(bf16[64,1024]{1,0:T(8,128)(2,1)} %param.11) | copy-start | bytes 393220
  550.7 386.3 %copy-start.5 = (f32[160]{0:T(256)S(1)}, f32[160]{0:T(256)}, u32[]{:S(2)}) copy-start(f32[160]{0:T(256)} %param.13) | copy-start | bytes 1924
  634.7 462.2 %all-gather.5.cloned.1.call-start = ((), (), s32[]{:S(2)}) async-start(), calls=%async_computation | async-start | bytes 4325376 | tf_op jit(solution)/shard_map/all_gather | solution.py:54
  635.5 622.5 %all-gather.7.cloned.1.call-start = ((), (), s32[]{:S(2)}) async-start(), calls=%async_computation.2 | async-start | bytes 4325376 | tf_op jit(solution)/shard_map/all_gather | solution.py:55
  1100.0 173.4 %copy-start.3 = (bf16[1024,512]{1,0:T(8,128)(2,1)S(1)}, bf16[1024,512]{1,0:T(8,128)(2,1)}, u32[]{:S(2)}) copy-start(bf16[1024,512]{1,0:T(8,128)(2,1)} %copy-done.2) | copy-start | bytes 3145732
Sparse Core Ops, SparseCore 0:
  9.2 532.3 all-gather.8
  634.9 302.1 all-reduce.2
  939.0 157.9 all-gather.4
  1098.7 159.1 all-gather.6
where the time goes:
time: 1290 us
  waiting for transfers between devices  1140 us (88%)
  blocking collectives  81.6 us (6%)
  matrix products  33.3 us (3%)
  between operations  13.2 us (1%)
    all_gather x1, waiting for transfers between devices, per_device(): lax.all_gather(batch_points, ('narrow', 'wide', 'nys'), axis=0, tiled=True)  524 us
    psum x1, waiting for transfers between devices, per_device(): projected = lax.psum(local_proj, ('narrow', 'nys'))  301 us
    all_gather x1, waiting for transfers between devices, per_device(): coefs = lax.all_gather(corrected, ('narrow', 'nys'), axis=0, tiled=True)  158 us
    all_gather x1, waiting for transfers between devices, per_device(): lax.all_gather(nystrom_points, ('narrow', 'nys'), axis=0, tiled=True)  158 us
    psum x1, blocking collectives, per_device(): lax.psum(partial_value - placed, ('narrow', 'wide', 'nys'))  81.6 us
  transfers between devices with their start and end apart: 4, of which 4 were waited for; matrix products, arithmetic and copies ran while one was open for 1% of the time, Pallas kernels for 0%

commit v1 on v0

--- a/solution.py
+++ b/solution.py
@@ -47,7 +47,13 @@
     local_proj = lax.dot_general(
         eigvecs, pulled, (((0,), (0,)), ((), ())), precision=lax.Precision.HIGHEST
     )
-    projected = lax.psum(local_proj, ("narrow", "nys"))
+
+    def clear_the_heaps(buf):
+        for h in ("nys", "narrow"):
+            buf = lax.psum(buf, h)
+        return buf
+
+    projected = clear_the_heaps(local_proj)
     scaled_proj = corrections[:, None] * projected
     gradient = jnp.dot(k_batch, residual, preferred_element_type=jnp.float32)
     corrected = jnp.dot(eigvecs, scaled_proj, precision=lax.Precision.HIGHEST).astype(jnp.bfloat16)

time: 1290 us -> 1040 us (0.81)
  waiting for transfers between devices: 1140 us -> 893 us
    psum x1 -> x2, waiting for transfers between devices: 301 us -> 134 us  [clear_the_heaps(): buf = lax.psum(buf, h)]
    all_gather x1, waiting for transfers between devices: 158 us -> 76.2 us  [per_device(): lax.all_gather(nystrom_points, ('narrow', 'nys'), axis=0, tiled=True)]
  transfers between devices with their start and end apart: 4 -> 5, of which waited for: 4 -> 5; matrix products, arithmetic and copies ran while one was open for 1% -> 2% of each run, Pallas kernels for 0% -> 0%
where the time goes in v1:
time: 1040 us
  waiting for transfers between devices  893 us (86%)
  blocking collectives  81.6 us (8%)
  matrix products  33.3 us (3%)
  between operations  14.7 us (1%)
    all_gather x1, waiting for transfers between devices, per_device(): lax.all_gather(batch_points, ('narrow', 'wide', 'nys'), axis=0, tiled=True)  524 us
    all_gather x1, waiting for transfers between devices, per_device(): coefs = lax.all_gather(corrected, ('narrow', 'nys'), axis=0, tiled=True)  158 us
    psum x2, waiting for transfers between devices, clear_the_heaps(): buf = lax.psum(buf, h)  134 us
    psum x1, blocking collectives, per_device(): lax.psum(partial_value - placed, ('narrow', 'wide', 'nys'))  81.6 us
    all_gather x1, waiting for transfers between devices, per_device(): lax.all_gather(nystrom_points, ('narrow', 'nys'), axis=0, tiled=True)  76.2 us
  transfers between devices with their start and end apart: 5, of which 5 were waited for; matrix products, arithmetic and copies ran while one was open for 2% of the time, Pallas kernels for 0%

profile of v1, /device:TPU:2, one launch (start us, length us, event | category | flops | bytes accessed | tf_op | source)
XLA Modules:
  0.0 1038.8 jit_solution(12629331509632987009)
XLA Ops:
  7.4 0.0 copy-start
  7.4 0.0 all-gather.9.cloned.1.call-start
  7.4 0.7 all-gather.9.cloned.1.call-update
  8.1 0.0 all-reduce.4.cloned.1.call-start
  8.1 0.9 copy.9
  9.1 0.2 broadcast_in_dim.2
  9.3 6.3 dynamic_update_slice.3
  15.6 1.0 multiply_reduce_fusion.3
  16.6 2.1 multiply_reduce_fusion.1
  18.7 523.6 %all-gather.9.cloned.1.call-done = bf16[256,2,1024]{2,1,0:T(2,128)(2,1)} async-done(((bf16[1,2,1024]{2,1,0:T(2,128)(2,1)}), bf16[256,2,1024]{2,1,0:T(2,128)(2,1)}) %all-gather.9.cloned.1.call-update) | async-done | bytes 1048592 | tf_op jit(solution)/shard_map/all_gather | solution.py:27
  542.3 1.5 reshape.6
  543.8 0.3 multiply_reduce_fusion.2
  544.1 0.0 copy-start.1
  544.1 3.8 exponential_convert_fusion.1
  547.9 0.0 copy-start.2
  547.9 1.1 copy-done.2
  549.0 0.0 copy-done.1
  549.0 0.0 copy-start.4
  549.0 2.6 multiply_subtract_fusion.1
  551.6 0.0 copy-start.5
  551.6 81.6 %all-reduce.7 = bf16[512,1000]{0,1:T(8,128)(2,1)S(1)} all-reduce(f32[512,1000]{0,1:T(8,128)} %multiply_subtract_fusion.1), channel_id=1, replica_groups=mesh['narrow'=8,'wide'=8,'nys'=4] {'narrow','wide','nys'}, use_global_device_ids=true, to_apply=%region_2.0 | all-reduce | flops 512000 | bytes 3072000 | tf_op jit(solution)/shard_map/psum | solution.py:44
  633.1 0.0 copy-done.4
  633.1 0.8 fusion.12
  634.0 0.0 copy-done
  634.0 1.6 convolution_bitcast_fusion
  635.5 0.0 all-reduce.4.cloned.1.call-update
  635.6 0.0 all-reduce.6.cloned.1.call-start
  635.6 46.4 %all-reduce.4.cloned.1.call-done = f32[160,1000]{1,0:T(8,128)} async-done(((f32[160,1000]{1,0:T(8,128)}), f32[160,1000]{1,0:T(8,128)}) %all-reduce.4.cloned.1.call-update) | async-done | bytes 640016 | tf_op jit(solution)/shard_map/psum | solution.py:53
  682.0 0.0 all-reduce.6.cloned.1.call-update
  682.0 0.0 all-gather.5.cloned.1.call-start
  682.1 0.5 all-gather.5.cloned.1.call-update
  682.6 0.2 all-gather.7.cloned.1.call-start
  682.8 87.5 %all-reduce.6.cloned.1.call-done = f32[160,1000]{1,0:T(8,128)} async-done(((f32[160,1000]{1,0:T(8,128)}), f32[160,1000]{1,0:T(8,128)}) %all-reduce.6.cloned.1.call-update) | async-done | bytes 640016 | tf_op jit(solution)/shard_map/psum | solution.py:53
  770.3 0.0 copy-done.5
  770.3 2.3 fusion.4
  772.7 0.0 all-gather.7.cloned.1.call-update
  772.7 76.2 %all-gather.5.cloned.1.call-done = bf16[2048,1024]{1,0:T(8,128)(2,1)} async-done(((bf16[64,1024]{1,0:T(8,128)(2,1)}), bf16[2048,1024]{1,0:T(8,128)(2,1)}) %all-gather.5.cloned.1.call-update) | async-done | bytes 4194320 | tf_op jit(solution)/shard_map/all_gather | solution.py:60
  848.9 3.1 multiply_reduce_fusion
  852.0 0.0 copy-start.3
  852.0 157.6 %all-gather.7.cloned.1.call-done = bf16[2048,1000]{1,0:T(8,128)(2,1)} async-done(((bf16[64,1000]{1,0:T(8,128)(2,1)}), bf16[2048,1000]{1,0:T(8,128)(2,1)}) %all-gather.7.cloned.1.call-update) | async-done | bytes 4096016 | tf_op jit(solution)/shard_map/all_gather | solution.py:61
  1009.6 15.5 %fusion.13 = f32[1024,1000]{0,1:T(8,128)} fusion(bf16[2048,1000]{1,0:T(8,128)(2,1)} %all-gather.7.cloned.1.call-done, bf16[1024,1024]{1,0:T(8,128)(2,1)} %param.7, bf16[2048,1024]{1,0:T(8,128)(2,1)} %all-gather.5.cloned.1.call-done, f32[2048]{0:T(1024)S(1)} %multiply_reduce_fusion, f32[1024]{0:T(1024)S(1)} %multiply_reduce_fusion.1), kind=kOutput, calls=%fused_computation.21 | convolution fusion | flops 8503951360 | bytes 14495744 | tf_op jit(solution)/shard_map/dot_general | solution.py:63
  1025.1 0.0 copy-done.3
  1025.1 6.7 multiply_subtract_fusion
Async XLA Ops:
  7.4 626.6 %copy-start = (f32[64,160]{1,0:T(8,128)S(1)}, f32[64,160]{1,0:T(8,128)}, u32[]{:S(2)}) copy-start(f32[64,160]{1,0:T(8,128)} %param.12) | copy-start | bytes 122884
  7.4 535.0 %all-gather.9.cloned.1.call-start = ((), (), s32[]{:S(2)}) async-start(), calls=%async_computation.4 | async-start | bytes 1052672 | tf_op jit(solution)/shard_map/all_gather | solution.py:27
  8.1 673.9 %all-reduce.4.cloned.1.call-start = ((), (), s32[]{:S(2)}) async-start(), calls=%async_computation.1 | async-start | bytes 1310720 | tf_op jit(solution)/shard_map/psum | solution.py:53
  544.1 4.9 copy-start.1
  547.9 1.1 copy-start.2
  549.0 84.1 %copy-start.4 = (bf16[64,1024]{1,0:T(8,128)(2,1)S(1)}, bf16[64,1024]{1,0:T(8,128)(2,1)}, u32[]{:S(2)}) copy-start(bf16[64,1024]{1,0:T(8,128)(2,1)} %param.11) | copy-start | bytes 393220
  551.6 218.8 %copy-start.5 = (f32[160]{0:T(256)S(1)}, f32[160]{0:T(256)}, u32[]{:S(2)}) copy-start(f32[160]{0:T(256)} %param.13) | copy-start | bytes 1924
  635.6 134.8 %all-reduce.6.cloned.1.call-start = ((), (), s32[]{:S(2)}) async-start(), calls=%async_computation.2 | async-start | bytes 1310720 | tf_op jit(solution)/shard_map/psum | solution.py:53
  682.0 166.9 %all-gather.5.cloned.1.call-start = ((), (), s32[]{:S(2)}) async-start(), calls=%async_computation | async-start | bytes 4325376 | tf_op jit(solution)/shard_map/all_gather | solution.py:60
  682.6 327.0 %all-gather.7.cloned.1.call-start = ((), (), s32[]{:S(2)}) async-start(), calls=%async_computation.3 | async-start | bytes 4325376 | tf_op jit(solution)/shard_map/all_gather | solution.py:61
  852.0 173.1 %copy-start.3 = (bf16[1024,512]{1,0:T(8,128)(2,1)S(1)}, bf16[1024,512]{1,0:T(8,128)(2,1)}, u32[]{:S(2)}) copy-start(bf16[1024,512]{1,0:T(8,128)(2,1)} %copy-done.2) | copy-start | bytes 3145732
Sparse Core Ops, SparseCore 0:
  10.0 532.3 all-gather.8
  635.7 46.2 all-reduce.3
  684.6 85.6 all-reduce.5
Sparse Core Ops, SparseCore 1:
  684.3 164.6 all-gather.4
  850.6 158.9 all-gather.6
